TPU v7x, 32 devices: a whole 2x2x4 slice. The times are simulated.
32 devices in a mesh: dp: 4 (over y, x), feat: 8 (over z, core).
Axes of the slice: x: 2, y: 2, z: 4, core: 2. Of those that a mesh axis runs over, the one named last changes fastest.
Arguments:
- features: bfloat16 [8192, 1024], P('dp', 'feat'), may hold values from -6 to 6
- owners: int32 [8, 64, 1], P('feat', 'dp'), may hold values from 0 to 3; in each aligned block of 16 rows (0 to 15, 16 to 31, ..., all dimensions but the last counted through in order) at most 8 rows name the same one
- weights: bfloat16 [8, 4096], P(None, ('dp', 'feat')), may hold values from -0.1875 to 0.1875
- labels: int32 [8192], P('dp'), may hold values from 0 to 7
Outputs:
- hessian: float32 [32, 1024, 1024], P(('dp', 'feat'))
- gradient: float32 [8, 4096], P(None, ('dp', 'feat'))
Inputs may be any that keep to these rules, and one draw needn't show every extreme that they name: `owners`: among the 16 row blocks of one index of dp, in one tile column, at most 8 name the same owner, a bound that some block reaches.
All inputs are finite; a program needn't handle non-finite values.
Results may differ from a plain program's by a relative error of at most 0.0023.
Values may be sent and summed in bfloat16 or wider, within the bound.
A program may use at most 64 MiB of HBM per device.

v0:
```python
import math
import jax
import jax.numpy as jnp
from jax import lax
from jax.sharding import PartitionSpec as P


def normalize(logits):
    expo = jnp.exp(logits)
    return expo / jnp.sum(expo, axis=-1, keepdims=True)


def spread_diagonal(diag_part, classes, width):
    blocks = diag_part.reshape(classes, width, width)
    unit = jnp.eye(classes, dtype=jnp.float32)
    return (unit[:, None, :, None] * blocks[:, :, None, :]).reshape(
        classes * width, classes * width
    )


def arrange(target, groups, capacity):
    count = target.shape[0]
    order = jnp.arange(count, dtype=jnp.int32)
    earlier = (order[None, :] < order[:, None]) & (target[None, :] == target[:, None])
    ranking = jnp.sum(earlier.astype(jnp.int32), axis=1)
    slot_index = jnp.arange(groups * capacity, dtype=jnp.int32)
    slot_group = slot_index // capacity
    slot_rank = slot_index % capacity
    hits = (target[None, :] == slot_group[:, None]) & (ranking[None, :] == slot_rank[:, None])
    source = jnp.sum(jnp.where(hits, order[None, :], 0), axis=1)
    filled = jnp.any(hits, axis=1)
    return (source, filled)


def select_blocks(block_data, source, filled):
    picked = jnp.take(block_data, source, axis=0)
    return jnp.where(filled[:, None, None], picked, jnp.zeros_like(picked))


def accumulate(totals, feature_rows, prob_rows, classes):
    count, width = feature_rows.shape
    group = math.gcd(count, 512)

    def turn(step, state):
        hess_acc, grad_acc = state
        begin = step * group
        x_part = lax.dynamic_slice_in_dim(feature_rows, begin, group, 0)
        p_part = lax.dynamic_slice_in_dim(prob_rows, begin, group, 0)
        probs = p_part[:, :classes].astype(jnp.float32)
        resid = p_part[:, classes:]
        kron_rows = (
            (probs[:, :, None] * x_part.astype(jnp.float32)[:, None, :])
            .reshape(group, classes * width)
            .astype(jnp.bfloat16)
        )
        joint = jnp.concatenate([kron_rows, x_part], axis=1)
        product = lax.dot_general(
            kron_rows, joint, (((0,), (0,)), ((), ())), preferred_element_type=jnp.float32
        )
        square = product[:, : classes * width]
        diag_part = product[:, classes * width :]
        grad_term = lax.dot_general(
            resid, x_part, (((0,), (0,)), ((), ())), preferred_element_type=jnp.float32
        )
        return (
            hess_acc + spread_diagonal(diag_part, classes, width) - square,
            grad_acc + grad_term,
        )

    return lax.fori_loop(0, count // group, turn, totals)


def per_device(features, owners, weights, labels):
    rows, width = features.shape
    classes = weights.shape[0]
    blocks = owners.shape[1]
    block_rows = rows // blocks
    dp_count = lax.axis_size("dp")
    capacity = max(2, 2 * ((blocks + dp_count - 1) // dp_count))
    target = owners.reshape(blocks)
    gathered = lax.all_gather(weights, "dp", axis=1, tiled=True)
    table = gathered.reshape(classes, dp_count, width)
    every_owner = jnp.einsum("rt,cut->ruc", features, table, preferred_element_type=jnp.float32)
    row_owner = jnp.repeat(target, block_rows)
    owner_mask = (row_owner[:, None] == jnp.arange(dp_count, dtype=jnp.int32)[None, :]).astype(
        jnp.float32
    )
    partial_logits = jnp.sum(every_owner * owner_mask[:, :, None], axis=1)
    logits = lax.psum(partial_logits, "feat")
    probs = normalize(logits)
    onehot = (labels[:, None] == jnp.arange(classes, dtype=jnp.int32)[None, :]).astype(jnp.float32)
    probs_half = probs.astype(jnp.bfloat16)
    resid = (probs - onehot).astype(jnp.bfloat16)
    paired = jnp.concatenate([probs_half, resid], axis=1)
    feature_blocks = features.reshape(blocks, block_rows, width)
    paired_blocks = paired.reshape(blocks, block_rows, 2 * classes)
    start = (
        jnp.zeros((classes * width, classes * width), jnp.float32),
        jnp.zeros((classes, width), jnp.float32),
    )
    source, filled = arrange(target, dp_count, capacity)
    sent_features = select_blocks(feature_blocks, source, filled)
    sent_paired = select_blocks(paired_blocks, source, filled)
    got_features, got_paired = (
        lax.all_to_all(sent_features, "dp", split_axis=0, concat_axis=0, tiled=True),
        lax.all_to_all(sent_paired, "dp", split_axis=0, concat_axis=0, tiled=True),
    )
    hess_acc, grad_acc = accumulate(
        start, got_features.reshape(-1, width), got_paired.reshape(-1, 2 * classes), classes
    )
    hessian = (hess_acc / block_rows)[None]
    gradient = grad_acc / block_rows
    return (hessian, gradient)


def solution(mesh):
    in_specs = (P("dp", "feat"), P("feat", "dp", None), P(None, ("dp", "feat")), P("dp"))
    out_specs = (P(("dp", "feat"), None, None), P(None, ("dp", "feat")))
    return jax.shard_map(
        per_device, mesh=mesh, in_specs=in_specs, out_specs=out_specs, check_vma=False
    )
```

profile of v0, /device:TPU:0, one launch (start us, length us, event | category | flops | bytes accessed | tf_op | source)
XLA Modules:
  0.0 189.6 jit_solution(15932147110795025760)
XLA Ops:
  7.2 0.8 broadcast_bitcast_fusion
  8.0 9.6 %all_gather.3 = bf16[8,512]{1,0:T(8,128)(2,1)S(1)} all-gather(bf16[8,128]{1,0:T(8,128)(2,1)} %param.8), channel_id=1, replica_groups=mesh['dp'=4,'feat'=8] {'dp'}, dimensions={1}, use_global_device_ids=true | all-gather | bytes 10240 | tf_op jit(solution)/shard_map/all_gather | solution.py:81
  17.7 0.9 fusion.9
  18.6 0.9 convert_reduce_fusion
  21.0 0.7 gather_fusion.1
  21.8 50.8 %all-reduce.2.cloned.1.call-done = f32[2048,8]{0,1:T(8,128)} async-done(((f32[2048,8]{0,1:T(8,128)}), f32[2048,8]{0,1:T(8,128)}) %all-reduce.2.cloned.1.call-update) | async-done | bytes 65552 | tf_op jit(solution)/shard_map/psum | solution.py:89
  72.6 0.9 exponential_reduce_fusion
  73.5 0.9 fusion.12
  75.0 0.8 select_select_fusion.1
  75.8 3.6 %all-to-all-start = ((bf16[32,128,16]{1,2,0:T(8,128)(2,1)}), bf16[32,128,16]{1,2,0:T(8,128)(2,1)S(1)}, u32[]{:S(2)}, u32[]{:S(2)}) async-start(bf16[32,128,16]{1,2,0:T(8,128)(2,1)} %select_select_fusion.1), calls=%async_computation | async-start | bytes 262144 | tf_op jit(solution)/shard_map/all_to_all | solution.py:106
  79.4 1.2 select_select_fusion
  80.6 3.8 %all-to-all-done = bf16[32,128,16]{1,2,0:T(8,128)(2,1)S(1)} async-done(((bf16[32,128,16]{1,2,0:T(8,128)(2,1)}), bf16[32,128,16]{1,2,0:T(8,128)(2,1)S(1)}, u32[]{:S(2)}, u32[]{:S(2)}) %all-to-all-start) | async-done | bytes 131104 | tf_op jit(solution)/shard_map/all_to_all | solution.py:106
  84.4 3.5 %all-to-all-start.1 = ((bf16[32,128,128]{2,1,0:T(8,128)(2,1)}), bf16[32,128,128]{2,1,0:T(8,128)(2,1)S(1)}, u32[]{:S(2)}, u32[]{:S(2)}) async-start(bf16[32,128,128]{2,1,0:T(8,128)(2,1)} %select_select_fusion), calls=%async_computation.1 | async-start | bytes 2097152 | tf_op jit(solution)/shard_map/all_to_all | solution.py:105
  88.0 10.9 %all-to-all-done.1 = bf16[32,128,128]{2,1,0:T(8,128)(2,1)S(1)} async-done(((bf16[32,128,128]{2,1,0:T(8,128)(2,1)}), bf16[32,128,128]{2,1,0:T(8,128)(2,1)S(1)}, u32[]{:S(2)}, u32[]{:S(2)}) %all-to-all-start.1) | async-done | bytes 1048608 | tf_op jit(solution)/shard_map/all_to_all | solution.py:105
  98.9 78.2 %while.16 = (s32[]{:T(128)}, f32[1024,1024]{1,0:T(8,128)}, f32[8,128]{1,0:T(8,128)S(1)}, bf16[4096,16]{0,1:T(8,128)(2,1)S(1)}, bf16[4096,128]{1,0:T(8,128)(2,1)S...) while((s32[]{:T(128)}, f32[1024,1024]{1,0:T(8,128)}, f32[8,128]{1,0:T(8,128)S(1)}, ...), condition=%wide.region_7.8_spmd.clone, body=%wide.region_6.7_spmd.clone.sunk | while | flops 1216682112 | bytes 66151160 | solution.py:70
  100.2 1.6 fusion.34
  102.2 1.8 copy-done.1
  103.9 2.7 %fusion.36 = f32[1024,1024]{1,0:T(8,128)S(1)} fusion(f32[128,8,8,128]{3,2,1,0:T(8,128)S(1)} %bitcast.61, f32[1024,1152]{1,0:T(8,128)S(1)} %fusion.34, f32[1024,1024]{1,0:T(8,128)S(1)} %copy-done.1, pred[]{:T(512)S(6)} %compare.8), kind=kLoop, calls=%fused_computation.3.clone.1 | loop fusion | flops 3145728 | bytes 16777216 | tf_op jit(solution)/shard_map/while/body/eval_jaxpr/sub | solution.py:66
  106.6 2.0 %copy-done.2 = f32[1024,1024]{1,0:T(8,128)} copy-done((f32[1024,1024]{1,0:T(8,128)}, f32[1024,1024]{1,0:T(8,128)S(1)}, u32[]{:S(2)}) %copy-start.2) | copy-done | bytes 4194328 | tf_op jit(solution)/shard_map/while
  109.9 1.6 fusion.34
  111.9 1.8 copy-done.1
  113.7 2.7 %fusion.36 = f32[1024,1024]{1,0:T(8,128)S(1)} fusion(f32[128,8,8,128]{3,2,1,0:T(8,128)S(1)} %bitcast.61, f32[1024,1152]{1,0:T(8,128)S(1)} %fusion.34, f32[1024,1024]{1,0:T(8,128)S(1)} %copy-done.1, pred[]{:T(512)S(6)} %compare.8), kind=kLoop, calls=%fused_computation.3.clone.1 | loop fusion | flops 3145728 | bytes 16777216 | tf_op jit(solution)/shard_map/while/body/eval_jaxpr/sub | solution.py:66
  116.4 2.0 %copy-done.2 = f32[1024,1024]{1,0:T(8,128)} copy-done((f32[1024,1024]{1,0:T(8,128)}, f32[1024,1024]{1,0:T(8,128)S(1)}, u32[]{:S(2)}) %copy-start.2) | copy-done | bytes 4194328 | tf_op jit(solution)/shard_map/while
  119.7 1.6 fusion.34
  121.7 1.8 copy-done.1
  123.5 2.7 %fusion.36 = f32[1024,1024]{1,0:T(8,128)S(1)} fusion(f32[128,8,8,128]{3,2,1,0:T(8,128)S(1)} %bitcast.61, f32[1024,1152]{1,0:T(8,128)S(1)} %fusion.34, f32[1024,1024]{1,0:T(8,128)S(1)} %copy-done.1, pred[]{:T(512)S(6)} %compare.8), kind=kLoop, calls=%fused_computation.3.clone.1 | loop fusion | flops 3145728 | bytes 16777216 | tf_op jit(solution)/shard_map/while/body/eval_jaxpr/sub | solution.py:66
  126.2 2.0 %copy-done.2 = f32[1024,1024]{1,0:T(8,128)} copy-done((f32[1024,1024]{1,0:T(8,128)}, f32[1024,1024]{1,0:T(8,128)S(1)}, u32[]{:S(2)}) %copy-start.2) | copy-done | bytes 4194328 | tf_op jit(solution)/shard_map/while
  129.5 1.6 fusion.34
  131.5 1.8 copy-done.1
  133.3 2.7 %fusion.36 = f32[1024,1024]{1,0:T(8,128)S(1)} fusion(f32[128,8,8,128]{3,2,1,0:T(8,128)S(1)} %bitcast.61, f32[1024,1152]{1,0:T(8,128)S(1)} %fusion.34, f32[1024,1024]{1,0:T(8,128)S(1)} %copy-done.1, pred[]{:T(512)S(6)} %compare.8), kind=kLoop, calls=%fused_computation.3.clone.1 | loop fusion | flops 3145728 | bytes 16777216 | tf_op jit(solution)/shard_map/while/body/eval_jaxpr/sub | solution.py:66
  136.0 2.0 %copy-done.2 = f32[1024,1024]{1,0:T(8,128)} copy-done((f32[1024,1024]{1,0:T(8,128)}, f32[1024,1024]{1,0:T(8,128)S(1)}, u32[]{:S(2)}) %copy-start.2) | copy-done | bytes 4194328 | tf_op jit(solution)/shard_map/while
  139.3 1.6 fusion.34
  141.3 1.8 copy-done.1
  143.1 2.7 %fusion.36 = f32[1024,1024]{1,0:T(8,128)S(1)} fusion(f32[128,8,8,128]{3,2,1,0:T(8,128)S(1)} %bitcast.61, f32[1024,1152]{1,0:T(8,128)S(1)} %fusion.34, f32[1024,1024]{1,0:T(8,128)S(1)} %copy-done.1, pred[]{:T(512)S(6)} %compare.8), kind=kLoop, calls=%fused_computation.3.clone.1 | loop fusion | flops 3145728 | bytes 16777216 | tf_op jit(solution)/shard_map/while/body/eval_jaxpr/sub | solution.py:66
  145.8 2.0 %copy-done.2 = f32[1024,1024]{1,0:T(8,128)} copy-done((f32[1024,1024]{1,0:T(8,128)}, f32[1024,1024]{1,0:T(8,128)S(1)}, u32[]{:S(2)}) %copy-start.2) | copy-done | bytes 4194328 | tf_op jit(solution)/shard_map/while
  149.1 1.6 fusion.34
  151.1 1.8 copy-done.1
  152.8 2.7 %fusion.36 = f32[1024,1024]{1,0:T(8,128)S(1)} fusion(f32[128,8,8,128]{3,2,1,0:T(8,128)S(1)} %bitcast.61, f32[1024,1152]{1,0:T(8,128)S(1)} %fusion.34, f32[1024,1024]{1,0:T(8,128)S(1)} %copy-done.1, pred[]{:T(512)S(6)} %compare.8), kind=kLoop, calls=%fused_computation.3.clone.1 | loop fusion | flops 3145728 | bytes 16777216 | tf_op jit(solution)/shard_map/while/body/eval_jaxpr/sub | solution.py:66
  155.5 2.0 %copy-done.2 = f32[1024,1024]{1,0:T(8,128)} copy-done((f32[1024,1024]{1,0:T(8,128)}, f32[1024,1024]{1,0:T(8,128)S(1)}, u32[]{:S(2)}) %copy-start.2) | copy-done | bytes 4194328 | tf_op jit(solution)/shard_map/while
  158.8 1.6 fusion.34
  160.9 1.8 copy-done.1
  162.6 2.7 %fusion.36 = f32[1024,1024]{1,0:T(8,128)S(1)} fusion(f32[128,8,8,128]{3,2,1,0:T(8,128)S(1)} %bitcast.61, f32[1024,1152]{1,0:T(8,128)S(1)} %fusion.34, f32[1024,1024]{1,0:T(8,128)S(1)} %copy-done.1, pred[]{:T(512)S(6)} %compare.8), kind=kLoop, calls=%fused_computation.3.clone.1 | loop fusion | flops 3145728 | bytes 16777216 | tf_op jit(solution)/shard_map/while/body/eval_jaxpr/sub | solution.py:66
  165.3 2.0 %copy-done.2 = f32[1024,1024]{1,0:T(8,128)} copy-done((f32[1024,1024]{1,0:T(8,128)}, f32[1024,1024]{1,0:T(8,128)S(1)}, u32[]{:S(2)}) %copy-start.2) | copy-done | bytes 4194328 | tf_op jit(solution)/shard_map/while
  168.6 1.6 fusion.34
  170.6 1.8 copy-done.1
  172.4 2.7 %fusion.36 = f32[1024,1024]{1,0:T(8,128)S(1)} fusion(f32[128,8,8,128]{3,2,1,0:T(8,128)S(1)} %bitcast.61, f32[1024,1152]{1,0:T(8,128)S(1)} %fusion.34, f32[1024,1024]{1,0:T(8,128)S(1)} %copy-done.1, pred[]{:T(512)S(6)} %compare.8), kind=kLoop, calls=%fused_computation.3.clone.1 | loop fusion | flops 3145728 | bytes 16777216 | tf_op jit(solution)/shard_map/while/body/eval_jaxpr/sub | solution.py:66
  175.1 2.0 %copy-done.2 = f32[1024,1024]{1,0:T(8,128)} copy-done((f32[1024,1024]{1,0:T(8,128)}, f32[1024,1024]{1,0:T(8,128)S(1)}, u32[]{:S(2)}) %copy-start.2) | copy-done | bytes 4194328 | tf_op jit(solution)/shard_map/while
  177.7 5.0 %multiply_bitcast_fusion = f32[1,1024,1024]{2,1,0:T(8,128)} fusion(f32[1024,1024]{1,0:T(8,128)} %get-tuple-element.97), kind=kLoop, calls=%fused_computation.18 | loop fusion | flops 1048576 | bytes 8388608 | tf_op jit(solution)/shard_map/broadcast_in_dim | solution.py:111
  (105 shorter events, 16.1 us)
Async XLA Ops:
  7.2 10.5 %copy-start = (bf16[2048,128]{1,0:T(8,128)(2,1)S(1)}, bf16[2048,128]{1,0:T(8,128)(2,1)}, u32[]{:S(2)}) copy-start(bf16[2048,128]{1,0:T(8,128)(2,1)} %param.6) | copy-start | bytes 1572868
  7.2 65.4 %all-reduce.2.cloned.1.call-start = ((), (), s32[]{:S(2)}) async-start(), calls=%async_computation.2 | async-start | bytes 131072 | tf_op jit(solution)/shard_map/psum | solution.py:89
  75.8 8.7 %all-to-all-start = ((bf16[32,128,16]{1,2,0:T(8,128)(2,1)}), bf16[32,128,16]{1,2,0:T(8,128)(2,1)S(1)}, u32[]{:S(2)}, u32[]{:S(2)}) async-start(bf16[32,128,16]{1,2,0:T(8,128)(2,1)} %select_select_fusion.1), calls=%async_computation | async-start | bytes 262144 | tf_op jit(solution)/shard_map/all_to_all | solution.py:106
  84.4 14.4 %all-to-all-start.1 = ((bf16[32,128,128]{2,1,0:T(8,128)(2,1)}), bf16[32,128,128]{2,1,0:T(8,128)(2,1)S(1)}, u32[]{:S(2)}, u32[]{:S(2)}) async-start(bf16[32,128,128]{2,1,0:T(8,128)(2,1)} %select_select_fusion), calls=%async_computation.1 | async-start | bytes 2097152 | tf_op jit(solution)/shard_map/all_to_all | solution.py:105
  101.7 2.2 %copy-start.1 = (f32[1024,1024]{1,0:T(8,128)S(1)}, f32[1024,1024]{1,0:T(8,128)}, u32[]{:S(2)}) copy-start(f32[1024,1024]{1,0:T(8,128)} %get-tuple-element.179) | copy-start | bytes 12582916 | tf_op jit(solution)/shard_map/while
  106.6 2.0 %copy-start.2 = (f32[1024,1024]{1,0:T(8,128)}, f32[1024,1024]{1,0:T(8,128)S(1)}, u32[]{:S(2)}) copy-start(f32[1024,1024]{1,0:T(8,128)S(1)} %fusion.36) | copy-start | bytes 12582916 | tf_op jit(solution)/shard_map/while
  111.5 2.2 %copy-start.1 = (f32[1024,1024]{1,0:T(8,128)S(1)}, f32[1024,1024]{1,0:T(8,128)}, u32[]{:S(2)}) copy-start(f32[1024,1024]{1,0:T(8,128)} %get-tuple-element.179) | copy-start | bytes 12582916 | tf_op jit(solution)/shard_map/while
  116.4 2.0 %copy-start.2 = (f32[1024,1024]{1,0:T(8,128)}, f32[1024,1024]{1,0:T(8,128)S(1)}, u32[]{:S(2)}) copy-start(f32[1024,1024]{1,0:T(8,128)S(1)} %fusion.36) | copy-start | bytes 12582916 | tf_op jit(solution)/shard_map/while
  121.3 2.2 %copy-start.1 = (f32[1024,1024]{1,0:T(8,128)S(1)}, f32[1024,1024]{1,0:T(8,128)}, u32[]{:S(2)}) copy-start(f32[1024,1024]{1,0:T(8,128)} %get-tuple-element.179) | copy-start | bytes 12582916 | tf_op jit(solution)/shard_map/while
  126.2 2.0 %copy-start.2 = (f32[1024,1024]{1,0:T(8,128)}, f32[1024,1024]{1,0:T(8,128)S(1)}, u32[]{:S(2)}) copy-start(f32[1024,1024]{1,0:T(8,128)S(1)} %fusion.36) | copy-start | bytes 12582916 | tf_op jit(solution)/shard_map/while
  131.1 2.2 %copy-start.1 = (f32[1024,1024]{1,0:T(8,128)S(1)}, f32[1024,1024]{1,0:T(8,128)}, u32[]{:S(2)}) copy-start(f32[1024,1024]{1,0:T(8,128)} %get-tuple-element.179) | copy-start | bytes 12582916 | tf_op jit(solution)/shard_map/while
  136.0 2.0 %copy-start.2 = (f32[1024,1024]{1,0:T(8,128)}, f32[1024,1024]{1,0:T(8,128)S(1)}, u32[]{:S(2)}) copy-start(f32[1024,1024]{1,0:T(8,128)S(1)} %fusion.36) | copy-start | bytes 12582916 | tf_op jit(solution)/shard_map/while
  140.9 2.2 %copy-start.1 = (f32[1024,1024]{1,0:T(8,128)S(1)}, f32[1024,1024]{1,0:T(8,128)}, u32[]{:S(2)}) copy-start(f32[1024,1024]{1,0:T(8,128)} %get-tuple-element.179) | copy-start | bytes 12582916 | tf_op jit(solution)/shard_map/while
  145.8 2.0 %copy-start.2 = (f32[1024,1024]{1,0:T(8,128)}, f32[1024,1024]{1,0:T(8,128)S(1)}, u32[]{:S(2)}) copy-start(f32[1024,1024]{1,0:T(8,128)S(1)} %fusion.36) | copy-start | bytes 12582916 | tf_op jit(solution)/shard_map/while
  150.6 2.2 %copy-start.1 = (f32[1024,1024]{1,0:T(8,128)S(1)}, f32[1024,1024]{1,0:T(8,128)}, u32[]{:S(2)}) copy-start(f32[1024,1024]{1,0:T(8,128)} %get-tuple-element.179) | copy-start | bytes 12582916 | tf_op jit(solution)/shard_map/while
  155.5 2.0 %copy-start.2 = (f32[1024,1024]{1,0:T(8,128)}, f32[1024,1024]{1,0:T(8,128)S(1)}, u32[]{:S(2)}) copy-start(f32[1024,1024]{1,0:T(8,128)S(1)} %fusion.36) | copy-start | bytes 12582916 | tf_op jit(solution)/shard_map/while
  160.4 2.2 %copy-start.1 = (f32[1024,1024]{1,0:T(8,128)S(1)}, f32[1024,1024]{1,0:T(8,128)}, u32[]{:S(2)}) copy-start(f32[1024,1024]{1,0:T(8,128)} %get-tuple-element.179) | copy-start | bytes 12582916 | tf_op jit(solution)/shard_map/while
  165.3 2.0 %copy-start.2 = (f32[1024,1024]{1,0:T(8,128)}, f32[1024,1024]{1,0:T(8,128)S(1)}, u32[]{:S(2)}) copy-start(f32[1024,1024]{1,0:T(8,128)S(1)} %fusion.36) | copy-start | bytes 12582916 | tf_op jit(solution)/shard_map/while
  170.2 2.2 %copy-start.1 = (f32[1024,1024]{1,0:T(8,128)S(1)}, f32[1024,1024]{1,0:T(8,128)}, u32[]{:S(2)}) copy-start(f32[1024,1024]{1,0:T(8,128)} %get-tuple-element.179) | copy-start | bytes 12582916 | tf_op jit(solution)/shard_map/while
  175.1 2.0 %copy-start.2 = (f32[1024,1024]{1,0:T(8,128)}, f32[1024,1024]{1,0:T(8,128)S(1)}, u32[]{:S(2)}) copy-start(f32[1024,1024]{1,0:T(8,128)S(1)} %fusion.36) | copy-start | bytes 12582916 | tf_op jit(solution)/shard_map/while
Sparse Core Ops, SparseCore 0:
  18.7 53.8 all-reduce.1
where the time goes:
time: 190 us
  waiting for transfers between devices  65.6 us (35%)
  other arithmetic  42.1 us (22%)
  local copies, waits for them, and re-layouts  35.8 us (19%)
  matrix products  14.6 us (8%)
  between operations  14.1 us (7%)
  blocking collectives  9.63 us (5%)
  starting transfers between devices  7.2 us (4%)
    psum x1, waiting for transfers between devices, per_device(): logits = lax.psum(partial_logits, 'feat')  50.8 us
    while x40, local copies, waits for them, and re-layouts  32.4 us
    sub x8, other arithmetic, turn(): hess_acc + spread_diagonal(diag_part, classes, width) - square  21.6 us
    dot_general x8, matrix products, turn(): lax.dot_general(kron_rows, joint, (((0,), (0,)), ((), ())), preferred_ele...  12.6 us
    all_to_all x1, waiting for transfers between devices, per_device(): lax.all_to_all(sent_features, 'dp', split_axis=0, concat_axis=0, tiled=True)  10.9 us
    all_gather x1, blocking collectives, per_device(): gathered = lax.all_gather(weights, 'dp', axis=1, tiled=True)  9.63 us
    convert_element_type x8, other arithmetic, turn(): kron_rows = (probs[:, :, None] * x_part.astype(jnp.float32)[:, None, :])....  5.53 us
    broadcast_in_dim x1, other arithmetic, per_device(): hessian = (hess_acc / block_rows)[None]  5.04 us
  transfers between devices with their start and end apart: 3, of which 3 were waited for; matrix products, arithmetic and copies ran while one was open for 2% of the time, Pallas kernels for 0%

commit v1 on v0

--- a/solution.py
+++ b/solution.py
@@ -3,6 +3,12 @@
 import jax.numpy as jnp
 from jax import lax
 from jax.sharding import PartitionSpec as P
+
+
+def add_all(value, mesh_axis):
+    blocks = lax.all_gather(value, mesh_axis, axis=0, tiled=False)
+    summed = blocks.sum(axis=0)
+    return summed
 
 
 def normalize(logits):
@@ -86,7 +92,7 @@
         jnp.float32
     )
     partial_logits = jnp.sum(every_owner * owner_mask[:, :, None], axis=1)
-    logits = lax.psum(partial_logits, "feat")
+    logits = add_all(partial_logits, "feat")
     probs = normalize(logits)
     onehot = (labels[:, None] == jnp.arange(classes, dtype=jnp.int32)[None, :]).astype(jnp.float32)
     probs_half = probs.astype(jnp.bfloat16)

time: 190 us -> 141 us (0.74)
  waiting for transfers between devices: 65.6 us -> 16.3 us
  blocking collectives: 9.63 us -> 25 us
  between operations: 14.1 us -> 0.73 us
    psum x1 -> x0, waiting for transfers between devices: 50.8 us -> none  [per_device(): logits = lax.psum(partial_logits, 'feat')]
    all_gather x0 -> x1, blocking collectives: none -> 15.4 us  [add_all(): blocks = lax.all_gather(value, mesh_axis, axis=0, tiled=False)]
    all_to_all x1, waiting for transfers between devices: 10.9 us -> 13.2 us  [per_device(): lax.all_to_all(sent_features, 'dp', split_axis=0, concat_axis=0, tiled=True)]
  transfers between devices with their start and end apart: 3 -> 2, of which waited for: 3 -> 2; matrix products, arithmetic and copies ran while one was open for 2% -> 1% of each run, Pallas kernels for 0% -> 0%
where the time goes in v1:
time: 141 us; the launch traced here: 140 us
  other arithmetic  41.2 us (29%)
  local copies, waits for them, and re-layouts  35.8 us (25%)
  blocking collectives  25 us (18%)
  waiting for transfers between devices  16.3 us (12%)
  matrix products  13.9 us (10%)
  starting transfers between devices  6.84 us (5%)
    while x40, local copies, waits for them, and re-layouts  32.4 us
    sub x8, other arithmetic, turn(): hess_acc + spread_diagonal(diag_part, classes, width) - square  21.6 us
    all_gather x1, blocking collectives, add_all(): blocks = lax.all_gather(value, mesh_axis, axis=0, tiled=False)  15.4 us
    all_to_all x1, waiting for transfers between devices, per_device(): lax.all_to_all(sent_features, 'dp', split_axis=0, concat_axis=0, tiled=True)  13.2 us
    dot_general x8, matrix products, turn(): lax.dot_general(kron_rows, joint, (((0,), (0,)), ((), ())), preferred_ele...  12.6 us
    all_gather x1, blocking collectives, per_device(): gathered = lax.all_gather(weights, 'dp', axis=1, tiled=True)  9.63 us
    convert_element_type x8, other arithmetic, turn(): kron_rows = (probs[:, :, None] * x_part.astype(jnp.float32)[:, None, :])....  5.53 us
    broadcast_in_dim x1, other arithmetic, per_device(): hessian = (hess_acc / block_rows)[None]  5.04 us
  transfers between devices with their start and end apart: 2, of which 2 were waited for; matrix products, arithmetic and copies ran while one was open for 1% of the time, Pallas kernels for 0%

profile of v1, /device:TPU:0, one launch (start us, length us, event | category | flops | bytes accessed | tf_op | source)
XLA Modules:
  0.0 140.4 jit_solution(6626834343008648804)
XLA Ops:
  0.7 0.9 convert_reduce_fusion
  1.6 0.7 select_reduce_fusion
  2.3 0.7 fusion.15
  3.1 0.7 broadcast_bitcast_fusion
  3.8 9.6 %all_gather.9 = bf16[8,512]{1,0:T(8,128)(2,1)S(1)} all-gather(bf16[8,128]{1,0:T(8,128)(2,1)} %param.8), channel_id=1, replica_groups=mesh['dp'=4,'feat'=8] {'dp'}, dimensions={1}, use_global_device_ids=true | all-gather | bytes 10240 | tf_op jit(solution)/shard_map/all_gather | solution.py:87
  13.7 15.4 %all-gather = f32[16384,8]{0,1:T(8,128)S(1)} all-gather(f32[2048,8]{0,1:T(8,128)S(1)} %fusion.9), channel_id=2, replica_groups=mesh['dp'=4,'feat'=8] {'feat'}, dimensions={0}, use_global_device_ids=true | all-gather | bytes 589824 | tf_op jit(solution)/shard_map/all_gather | solution.py:9
  29.2 0.7 fusion.11
  30.6 0.8 select_select_fusion.1
  31.4 3.3 %all-to-all-start = ((bf16[32,128,16]{1,2,0:T(8,128)(2,1)}), bf16[32,128,16]{1,2,0:T(8,128)(2,1)S(1)}, u32[]{:S(2)}, u32[]{:S(2)}) async-start(bf16[32,128,16]{1,2,0:T(8,128)(2,1)} %select_select_fusion.1), calls=%async_computation | async-start | bytes 262144 | tf_op jit(solution)/shard_map/all_to_all | solution.py:112
  34.7 0.7 gather_fusion.1
  35.4 1.2 select_select_fusion
  36.6 3.1 %all-to-all-done = bf16[32,128,16]{1,2,0:T(8,128)(2,1)S(1)} async-done(((bf16[32,128,16]{1,2,0:T(8,128)(2,1)}), bf16[32,128,16]{1,2,0:T(8,128)(2,1)S(1)}, u32[]{:S(2)}, u32[]{:S(2)}) %all-to-all-start) | async-done | bytes 131104 | tf_op jit(solution)/shard_map/all_to_all | solution.py:112
  39.8 3.5 %all-to-all-start.1 = ((bf16[32,128,128]{2,1,0:T(8,128)(2,1)}), bf16[32,128,128]{2,1,0:T(8,128)(2,1)S(1)}, u32[]{:S(2)}, u32[]{:S(2)}) async-start(bf16[32,128,128]{2,1,0:T(8,128)(2,1)} %select_select_fusion), calls=%async_computation.1 | async-start | bytes 2097152 | tf_op jit(solution)/shard_map/all_to_all | solution.py:111
  43.3 13.2 %all-to-all-done.1 = bf16[32,128,128]{2,1,0:T(8,128)(2,1)S(1)} async-done(((bf16[32,128,128]{2,1,0:T(8,128)(2,1)}), bf16[32,128,128]{2,1,0:T(8,128)(2,1)S(1)}, u32[]{:S(2)}, u32[]{:S(2)}) %all-to-all-start.1) | async-done | bytes 1048608 | tf_op jit(solution)/shard_map/all_to_all | solution.py:111
  56.5 78.2 %while.16 = (s32[]{:T(128)}, f32[1024,1024]{1,0:T(8,128)}, f32[8,128]{1,0:T(8,128)S(1)}, bf16[4096,16]{0,1:T(8,128)(2,1)S(1)}, bf16[4096,128]{1,0:T(8,128)(2,1)S...) while((s32[]{:T(128)}, f32[1024,1024]{1,0:T(8,128)}, f32[8,128]{1,0:T(8,128)S(1)}, ...), condition=%wide.region_7.8_spmd.clone, body=%wide.region_6.7_spmd.clone.sunk | while | flops 1216682112 | bytes 66151160 | solution.py:76
  57.8 1.6 %fusion.34 = f32[1024,1152]{1,0:T(8,128)S(1)} fusion(bf16[512,1024]{1,0:T(8,128)(2,1)S(1)} %bitcast.68, bf16[512,128]{1,0:T(8,128)(2,1)S(1)} %get-tuple-element.167), kind=kOutput, calls=%fused_computation.6.clone.1 | convolution fusion | flops 1210318848 | bytes 5898240 | tf_op jit(solution)/shard_map/while/body/eval_jaxpr/dot_general | solution.py:63
  59.8 1.8 %copy-done.1 = f32[1024,1024]{1,0:T(8,128)S(1)} copy-done((f32[1024,1024]{1,0:T(8,128)S(1)}, f32[1024,1024]{1,0:T(8,128)}, u32[]{:S(2)}) %copy-start.1) | copy-done | bytes 4194328 | tf_op jit(solution)/shard_map/while
  61.6 2.7 %fusion.36 = f32[1024,1024]{1,0:T(8,128)S(1)} fusion(f32[128,8,8,128]{3,2,1,0:T(8,128)S(1)} %bitcast.65, f32[1024,1152]{1,0:T(8,128)S(1)} %fusion.34, f32[1024,1024]{1,0:T(8,128)S(1)} %copy-done.1, pred[]{:T(512)S(6)} %compare.8), kind=kLoop, calls=%fused_computation.3.clone.1 | loop fusion | flops 3145728 | bytes 16777216 | tf_op jit(solution)/shard_map/while/body/eval_jaxpr/sub | solution.py:72
  64.3 2.0 %copy-done.2 = f32[1024,1024]{1,0:T(8,128)} copy-done((f32[1024,1024]{1,0:T(8,128)}, f32[1024,1024]{1,0:T(8,128)S(1)}, u32[]{:S(2)}) %copy-start.2) | copy-done | bytes 4194328 | tf_op jit(solution)/shard_map/while
  67.6 1.6 %fusion.34 = f32[1024,1152]{1,0:T(8,128)S(1)} fusion(bf16[512,1024]{1,0:T(8,128)(2,1)S(1)} %bitcast.68, bf16[512,128]{1,0:T(8,128)(2,1)S(1)} %get-tuple-element.167), kind=kOutput, calls=%fused_computation.6.clone.1 | convolution fusion | flops 1210318848 | bytes 5898240 | tf_op jit(solution)/shard_map/while/body/eval_jaxpr/dot_general | solution.py:63
  69.6 1.8 %copy-done.1 = f32[1024,1024]{1,0:T(8,128)S(1)} copy-done((f32[1024,1024]{1,0:T(8,128)S(1)}, f32[1024,1024]{1,0:T(8,128)}, u32[]{:S(2)}) %copy-start.1) | copy-done | bytes 4194328 | tf_op jit(solution)/shard_map/while
  71.4 2.7 %fusion.36 = f32[1024,1024]{1,0:T(8,128)S(1)} fusion(f32[128,8,8,128]{3,2,1,0:T(8,128)S(1)} %bitcast.65, f32[1024,1152]{1,0:T(8,128)S(1)} %fusion.34, f32[1024,1024]{1,0:T(8,128)S(1)} %copy-done.1, pred[]{:T(512)S(6)} %compare.8), kind=kLoop, calls=%fused_computation.3.clone.1 | loop fusion | flops 3145728 | bytes 16777216 | tf_op jit(solution)/shard_map/while/body/eval_jaxpr/sub | solution.py:72
  74.1 2.0 %copy-done.2 = f32[1024,1024]{1,0:T(8,128)} copy-done((f32[1024,1024]{1,0:T(8,128)}, f32[1024,1024]{1,0:T(8,128)S(1)}, u32[]{:S(2)}) %copy-start.2) | copy-done | bytes 4194328 | tf_op jit(solution)/shard_map/while
  77.4 1.6 %fusion.34 = f32[1024,1152]{1,0:T(8,128)S(1)} fusion(bf16[512,1024]{1,0:T(8,128)(2,1)S(1)} %bitcast.68, bf16[512,128]{1,0:T(8,128)(2,1)S(1)} %get-tuple-element.167), kind=kOutput, calls=%fused_computation.6.clone.1 | convolution fusion | flops 1210318848 | bytes 5898240 | tf_op jit(solution)/shard_map/while/body/eval_jaxpr/dot_general | solution.py:63
  79.4 1.8 %copy-done.1 = f32[1024,1024]{1,0:T(8,128)S(1)} copy-done((f32[1024,1024]{1,0:T(8,128)S(1)}, f32[1024,1024]{1,0:T(8,128)}, u32[]{:S(2)}) %copy-start.1) | copy-done | bytes 4194328 | tf_op jit(solution)/shard_map/while
  81.1 2.7 %fusion.36 = f32[1024,1024]{1,0:T(8,128)S(1)} fusion(f32[128,8,8,128]{3,2,1,0:T(8,128)S(1)} %bitcast.65, f32[1024,1152]{1,0:T(8,128)S(1)} %fusion.34, f32[1024,1024]{1,0:T(8,128)S(1)} %copy-done.1, pred[]{:T(512)S(6)} %compare.8), kind=kLoop, calls=%fused_computation.3.clone.1 | loop fusion | flops 3145728 | bytes 16777216 | tf_op jit(solution)/shard_map/while/body/eval_jaxpr/sub | solution.py:72
  83.9 2.0 %copy-done.2 = f32[1024,1024]{1,0:T(8,128)} copy-done((f32[1024,1024]{1,0:T(8,128)}, f32[1024,1024]{1,0:T(8,128)S(1)}, u32[]{:S(2)}) %copy-start.2) | copy-done | bytes 4194328 | tf_op jit(solution)/shard_map/while
  87.2 1.6 %fusion.34 = f32[1024,1152]{1,0:T(8,128)S(1)} fusion(bf16[512,1024]{1,0:T(8,128)(2,1)S(1)} %bitcast.68, bf16[512,128]{1,0:T(8,128)(2,1)S(1)} %get-tuple-element.167), kind=kOutput, calls=%fused_computation.6.clone.1 | convolution fusion | flops 1210318848 | bytes 5898240 | tf_op jit(solution)/shard_map/while/body/eval_jaxpr/dot_general | solution.py:63
  89.2 1.8 %copy-done.1 = f32[1024,1024]{1,0:T(8,128)S(1)} copy-done((f32[1024,1024]{1,0:T(8,128)S(1)}, f32[1024,1024]{1,0:T(8,128)}, u32[]{:S(2)}) %copy-start.1) | copy-done | bytes 4194328 | tf_op jit(solution)/shard_map/while
  90.9 2.7 %fusion.36 = f32[1024,1024]{1,0:T(8,128)S(1)} fusion(f32[128,8,8,128]{3,2,1,0:T(8,128)S(1)} %bitcast.65, f32[1024,1152]{1,0:T(8,128)S(1)} %fusion.34, f32[1024,1024]{1,0:T(8,128)S(1)} %copy-done.1, pred[]{:T(512)S(6)} %compare.8), kind=kLoop, calls=%fused_computation.3.clone.1 | loop fusion | flops 3145728 | bytes 16777216 | tf_op jit(solution)/shard_map/while/body/eval_jaxpr/sub | solution.py:72
  93.6 2.0 %copy-done.2 = f32[1024,1024]{1,0:T(8,128)} copy-done((f32[1024,1024]{1,0:T(8,128)}, f32[1024,1024]{1,0:T(8,128)S(1)}, u32[]{:S(2)}) %copy-start.2) | copy-done | bytes 4194328 | tf_op jit(solution)/shard_map/while
  96.9 1.6 %fusion.34 = f32[1024,1152]{1,0:T(8,128)S(1)} fusion(bf16[512,1024]{1,0:T(8,128)(2,1)S(1)} %bitcast.68, bf16[512,128]{1,0:T(8,128)(2,1)S(1)} %get-tuple-element.167), kind=kOutput, calls=%fused_computation.6.clone.1 | convolution fusion | flops 1210318848 | bytes 5898240 | tf_op jit(solution)/shard_map/while/body/eval_jaxpr/dot_general | solution.py:63
  98.9 1.8 %copy-done.1 = f32[1024,1024]{1,0:T(8,128)S(1)} copy-done((f32[1024,1024]{1,0:T(8,128)S(1)}, f32[1024,1024]{1,0:T(8,128)}, u32[]{:S(2)}) %copy-start.1) | copy-done | bytes 4194328 | tf_op jit(solution)/shard_map/while
  100.7 2.7 %fusion.36 = f32[1024,1024]{1,0:T(8,128)S(1)} fusion(f32[128,8,8,128]{3,2,1,0:T(8,128)S(1)} %bitcast.65, f32[1024,1152]{1,0:T(8,128)S(1)} %fusion.34, f32[1024,1024]{1,0:T(8,128)S(1)} %copy-done.1, pred[]{:T(512)S(6)} %compare.8), kind=kLoop, calls=%fused_computation.3.clone.1 | loop fusion | flops 3145728 | bytes 16777216 | tf_op jit(solution)/shard_map/while/body/eval_jaxpr/sub | solution.py:72
  103.4 2.0 %copy-done.2 = f32[1024,1024]{1,0:T(8,128)} copy-done((f32[1024,1024]{1,0:T(8,128)}, f32[1024,1024]{1,0:T(8,128)S(1)}, u32[]{:S(2)}) %copy-start.2) | copy-done | bytes 4194328 | tf_op jit(solution)/shard_map/while
  106.7 1.6 %fusion.34 = f32[1024,1152]{1,0:T(8,128)S(1)} fusion(bf16[512,1024]{1,0:T(8,128)(2,1)S(1)} %bitcast.68, bf16[512,128]{1,0:T(8,128)(2,1)S(1)} %get-tuple-element.167), kind=kOutput, calls=%fused_computation.6.clone.1 | convolution fusion | flops 1210318848 | bytes 5898240 | tf_op jit(solution)/shard_map/while/body/eval_jaxpr/dot_general | solution.py:63
  108.7 1.8 %copy-done.1 = f32[1024,1024]{1,0:T(8,128)S(1)} copy-done((f32[1024,1024]{1,0:T(8,128)S(1)}, f32[1024,1024]{1,0:T(8,128)}, u32[]{:S(2)}) %copy-start.1) | copy-done | bytes 4194328 | tf_op jit(solution)/shard_map/while
  110.5 2.7 %fusion.36 = f32[1024,1024]{1,0:T(8,128)S(1)} fusion(f32[128,8,8,128]{3,2,1,0:T(8,128)S(1)} %bitcast.65, f32[1024,1152]{1,0:T(8,128)S(1)} %fusion.34, f32[1024,1024]{1,0:T(8,128)S(1)} %copy-done.1, pred[]{:T(512)S(6)} %compare.8), kind=kLoop, calls=%fused_computation.3.clone.1 | loop fusion | flops 3145728 | bytes 16777216 | tf_op jit(solution)/shard_map/while/body/eval_jaxpr/sub | solution.py:72
  113.2 2.0 %copy-done.2 = f32[1024,1024]{1,0:T(8,128)} copy-done((f32[1024,1024]{1,0:T(8,128)}, f32[1024,1024]{1,0:T(8,128)S(1)}, u32[]{:S(2)}) %copy-start.2) | copy-done | bytes 4194328 | tf_op jit(solution)/shard_map/while
  116.5 1.6 %fusion.34 = f32[1024,1152]{1,0:T(8,128)S(1)} fusion(bf16[512,1024]{1,0:T(8,128)(2,1)S(1)} %bitcast.68, bf16[512,128]{1,0:T(8,128)(2,1)S(1)} %get-tuple-element.167), kind=kOutput, calls=%fused_computation.6.clone.1 | convolution fusion | flops 1210318848 | bytes 5898240 | tf_op jit(solution)/shard_map/while/body/eval_jaxpr/dot_general | solution.py:63
  118.5 1.8 %copy-done.1 = f32[1024,1024]{1,0:T(8,128)S(1)} copy-done((f32[1024,1024]{1,0:T(8,128)S(1)}, f32[1024,1024]{1,0:T(8,128)}, u32[]{:S(2)}) %copy-start.1) | copy-done | bytes 4194328 | tf_op jit(solution)/shard_map/while
  120.3 2.7 %fusion.36 = f32[1024,1024]{1,0:T(8,128)S(1)} fusion(f32[128,8,8,128]{3,2,1,0:T(8,128)S(1)} %bitcast.65, f32[1024,1152]{1,0:T(8,128)S(1)} %fusion.34, f32[1024,1024]{1,0:T(8,128)S(1)} %copy-done.1, pred[]{:T(512)S(6)} %compare.8), kind=kLoop, calls=%fused_computation.3.clone.1 | loop fusion | flops 3145728 | bytes 16777216 | tf_op jit(solution)/shard_map/while/body/eval_jaxpr/sub | solution.py:72
  123.0 2.0 %copy-done.2 = f32[1024,1024]{1,0:T(8,128)} copy-done((f32[1024,1024]{1,0:T(8,128)}, f32[1024,1024]{1,0:T(8,128)S(1)}, u32[]{:S(2)}) %copy-start.2) | copy-done | bytes 4194328 | tf_op jit(solution)/shard_map/while
  126.3 1.6 %fusion.34 = f32[1024,1152]{1,0:T(8,128)S(1)} fusion(bf16[512,1024]{1,0:T(8,128)(2,1)S(1)} %bitcast.68, bf16[512,128]{1,0:T(8,128)(2,1)S(1)} %get-tuple-element.167), kind=kOutput, calls=%fused_computation.6.clone.1 | convolution fusion | flops 1210318848 | bytes 5898240 | tf_op jit(solution)/shard_map/while/body/eval_jaxpr/dot_general | solution.py:63
  128.3 1.8 %copy-done.1 = f32[1024,1024]{1,0:T(8,128)S(1)} copy-done((f32[1024,1024]{1,0:T(8,128)S(1)}, f32[1024,1024]{1,0:T(8,128)}, u32[]{:S(2)}) %copy-start.1) | copy-done | bytes 4194328 | tf_op jit(solution)/shard_map/while
  130.0 2.7 %fusion.36 = f32[1024,1024]{1,0:T(8,128)S(1)} fusion(f32[128,8,8,128]{3,2,1,0:T(8,128)S(1)} %bitcast.65, f32[1024,1152]{1,0:T(8,128)S(1)} %fusion.34, f32[1024,1024]{1,0:T(8,128)S(1)} %copy-done.1, pred[]{:T(512)S(6)} %compare.8), kind=kLoop, calls=%fused_computation.3.clone.1 | loop fusion | flops 3145728 | bytes 16777216 | tf_op jit(solution)/shard_map/while/body/eval_jaxpr/sub | solution.py:72
  132.8 2.0 %copy-done.2 = f32[1024,1024]{1,0:T(8,128)} copy-done((f32[1024,1024]{1,0:T(8,128)}, f32[1024,1024]{1,0:T(8,128)S(1)}, u32[]{:S(2)}) %copy-start.2) | copy-done | bytes 4194328 | tf_op jit(solution)/shard_map/while
  135.4 5.0 %multiply_bitcast_fusion = f32[1,1024,1024]{2,1,0:T(8,128)} fusion(f32[1024,1024]{1,0:T(8,128)} %get-tuple-element.97), kind=kLoop, calls=%fused_computation.18 | loop fusion | flops 1048576 | bytes 8388608 | tf_op jit(solution)/shard_map/broadcast_in_dim | solution.py:117
  (104 shorter events, 14.9 us)
Async XLA Ops:
  0.6 12.8 %copy-start = (bf16[2048,128]{1,0:T(8,128)(2,1)S(1)}, bf16[2048,128]{1,0:T(8,128)(2,1)}, u32[]{:S(2)}) copy-start(bf16[2048,128]{1,0:T(8,128)(2,1)} %param.6) | copy-start | bytes 1572868
  31.4 8.4 %all-to-all-start = ((bf16[32,128,16]{1,2,0:T(8,128)(2,1)}), bf16[32,128,16]{1,2,0:T(8,128)(2,1)S(1)}, u32[]{:S(2)}, u32[]{:S(2)}) async-start(bf16[32,128,16]{1,2,0:T(8,128)(2,1)} %select_select_fusion.1), calls=%async_computation | async-start | bytes 262144 | tf_op jit(solution)/shard_map/all_to_all | solution.py:112
  39.8 16.8 %all-to-all-start.1 = ((bf16[32,128,128]{2,1,0:T(8,128)(2,1)}), bf16[32,128,128]{2,1,0:T(8,128)(2,1)S(1)}, u32[]{:S(2)}, u32[]{:S(2)}) async-start(bf16[32,128,128]{2,1,0:T(8,128)(2,1)} %select_select_fusion), calls=%async_computation.1 | async-start | bytes 2097152 | tf_op jit(solution)/shard_map/all_to_all | solution.py:111
  59.4 2.2 %copy-start.1 = (f32[1024,1024]{1,0:T(8,128)S(1)}, f32[1024,1024]{1,0:T(8,128)}, u32[]{:S(2)}) copy-start(f32[1024,1024]{1,0:T(8,128)} %get-tuple-element.179) | copy-start | bytes 12582916 | tf_op jit(solution)/shard_map/while
  64.3 2.0 %copy-start.2 = (f32[1024,1024]{1,0:T(8,128)}, f32[1024,1024]{1,0:T(8,128)S(1)}, u32[]{:S(2)}) copy-start(f32[1024,1024]{1,0:T(8,128)S(1)} %fusion.36) | copy-start | bytes 12582916 | tf_op jit(solution)/shard_map/while
  69.2 2.2 %copy-start.1 = (f32[1024,1024]{1,0:T(8,128)S(1)}, f32[1024,1024]{1,0:T(8,128)}, u32[]{:S(2)}) copy-start(f32[1024,1024]{1,0:T(8,128)} %get-tuple-element.179) | copy-start | bytes 12582916 | tf_op jit(solution)/shard_map/while
  74.1 2.0 %copy-start.2 = (f32[1024,1024]{1,0:T(8,128)}, f32[1024,1024]{1,0:T(8,128)S(1)}, u32[]{:S(2)}) copy-start(f32[1024,1024]{1,0:T(8,128)S(1)} %fusion.36) | copy-start | bytes 12582916 | tf_op jit(solution)/shard_map/while
  79.0 2.2 %copy-start.1 = (f32[1024,1024]{1,0:T(8,128)S(1)}, f32[1024,1024]{1,0:T(8,128)}, u32[]{:S(2)}) copy-start(f32[1024,1024]{1,0:T(8,128)} %get-tuple-element.179) | copy-start | bytes 12582916 | tf_op jit(solution)/shard_map/while
  83.8 2.0 %copy-start.2 = (f32[1024,1024]{1,0:T(8,128)}, f32[1024,1024]{1,0:T(8,128)S(1)}, u32[]{:S(2)}) copy-start(f32[1024,1024]{1,0:T(8,128)S(1)} %fusion.36) | copy-start | bytes 12582916 | tf_op jit(solution)/shard_map/while
  88.7 2.2 %copy-start.1 = (f32[1024,1024]{1,0:T(8,128)S(1)}, f32[1024,1024]{1,0:T(8,128)}, u32[]{:S(2)}) copy-start(f32[1024,1024]{1,0:T(8,128)} %get-tuple-element.179) | copy-start | bytes 12582916 | tf_op jit(solution)/shard_map/while
  93.6 2.0 %copy-start.2 = (f32[1024,1024]{1,0:T(8,128)}, f32[1024,1024]{1,0:T(8,128)S(1)}, u32[]{:S(2)}) copy-start(f32[1024,1024]{1,0:T(8,128)S(1)} %fusion.36) | copy-start | bytes 12582916 | tf_op jit(solution)/shard_map/while
  98.5 2.2 %copy-start.1 = (f32[1024,1024]{1,0:T(8,128)S(1)}, f32[1024,1024]{1,0:T(8,128)}, u32[]{:S(2)}) copy-start(f32[1024,1024]{1,0:T(8,128)} %get-tuple-element.179) | copy-start | bytes 12582916 | tf_op jit(solution)/shard_map/while
  103.4 2.0 %copy-start.2 = (f32[1024,1024]{1,0:T(8,128)}, f32[1024,1024]{1,0:T(8,128)S(1)}, u32[]{:S(2)}) copy-start(f32[1024,1024]{1,0:T(8,128)S(1)} %fusion.36) | copy-start | bytes 12582916 | tf_op jit(solution)/shard_map/while
  108.3 2.2 %copy-start.1 = (f32[1024,1024]{1,0:T(8,128)S(1)}, f32[1024,1024]{1,0:T(8,128)}, u32[]{:S(2)}) copy-start(f32[1024,1024]{1,0:T(8,128)} %get-tuple-element.179) | copy-start | bytes 12582916 | tf_op jit(solution)/shard_map/while
  113.2 2.0 %copy-start.2 = (f32[1024,1024]{1,0:T(8,128)}, f32[1024,1024]{1,0:T(8,128)S(1)}, u32[]{:S(2)}) copy-start(f32[1024,1024]{1,0:T(8,128)S(1)} %fusion.36) | copy-start | bytes 12582916 | tf_op jit(solution)/shard_map/while
  118.1 2.2 %copy-start.1 = (f32[1024,1024]{1,0:T(8,128)S(1)}, f32[1024,1024]{1,0:T(8,128)}, u32[]{:S(2)}) copy-start(f32[1024,1024]{1,0:T(8,128)} %get-tuple-element.179) | copy-start | bytes 12582916 | tf_op jit(solution)/shard_map/while
  123.0 2.0 %copy-start.2 = (f32[1024,1024]{1,0:T(8,128)}, f32[1024,1024]{1,0:T(8,128)S(1)}, u32[]{:S(2)}) copy-start(f32[1024,1024]{1,0:T(8,128)S(1)} %fusion.36) | copy-start | bytes 12582916 | tf_op jit(solution)/shard_map/while
  127.9 2.2 %copy-start.1 = (f32[1024,1024]{1,0:T(8,128)S(1)}, f32[1024,1024]{1,0:T(8,128)}, u32[]{:S(2)}) copy-start(f32[1024,1024]{1,0:T(8,128)} %get-tuple-element.179) | copy-start | bytes 12582916 | tf_op jit(solution)/shard_map/while
  132.7 2.0 %copy-start.2 = (f32[1024,1024]{1,0:T(8,128)}, f32[1024,1024]{1,0:T(8,128)S(1)}, u32[]{:S(2)}) copy-start(f32[1024,1024]{1,0:T(8,128)S(1)} %fusion.36) | copy-start | bytes 12582916 | tf_op jit(solution)/shard_map/while
